TPU v7x, 32 devices: a whole 2x2x4 slice. The times are simulated.
32 devices in a mesh: shot: 2 (over y), gx: 4 (over z), sec: 2 (over x), gy: 2 (over core).
Axes of the slice: x: 2, y: 2, z: 4, core: 2. Of those that a mesh axis runs over, the one named last changes fastest.
Arguments:
- source_fields: float32 [8, 16, 32, 256], P('shot', 'sec', 'gx', 'gy'), parts along dimension 0, may hold values from -6 to 6
- receiver_fields: float32 [8, 16, 32, 256], P('shot', 'sec', 'gx', 'gy'), parts along dimension 0, may hold values from -6 to 6
- courant: float32 [16, 32, 256], P('sec', 'gx', 'gy'), may hold values from 0.05 to 0.15
- epsilon: float32 [16, 32, 256], P('sec', 'gx', 'gy'), may hold values from 0.05 to 0.3
- delta_param: float32 [16, 32, 256], P('sec', 'gx', 'gy'), may hold values from 0 to 0.15
- tilt_angle: float32 [16, 32, 256], P('sec', 'gx', 'gy'), may hold values from -0.8 to 0.8
- source_pos: int32 [6], P('shot'), parts along dimension 0, may hold values from 0 to 255, as said below
- wavelet: float32 [18], P('shot'), parts along dimension 0, may hold values from -24 to 24
- receiver_pos: int32 [512, 3], P('shot'), parts along dimension 0, may hold values from 0 to 255, as said below
- receiver_data: float32 [18, 256], P('shot'), parts along dimension 0, may hold values from -6 to 6
- step_counts: int32 [3], replicated, may hold values from 1 to 3, as said below
- offset_lags: int32 [48, 2], replicated, may hold values from -8 to 8, as said below
Outputs:
- offset_images: bfloat16 [96, 16, 32, 256], P('shot', 'sec', 'gx', 'gy'), parts along dimension 0
- source_out: float32 [8, 16, 32, 256], P('shot', 'sec', 'gx', 'gy'), parts along dimension 0
- receiver_out: float32 [8, 16, 32, 256], P('shot', 'sec', 'gx', 'gy'), parts along dimension 0
There are 2 independent parts, one for each index of `shot`. A program takes and returns all parts, laid end to end along the dimension named above; an argument that names none is the same for every part. Nothing has to cross between parts.
Inputs may be any that keep to these rules, and one draw needn't show every extreme that they name: `source_pos`: a grid cell: depth below 16, first horizontal below 32, second horizontal below 256; it lies on the last cell of the longest grid dimension and on cell 0 of another dimension. `receiver_pos`: grid cells: depth below 16, first horizontal below 32, second horizontal below 256; one receiver sits at the far corner of the grid and one at its anchor. `step_counts`: some snapshot takes all 3 steps. `offset_lags`: in each dimension some lag is 8 and some is minus 8.
All inputs are finite; a program needn't handle non-finite values.
Results may differ from a plain program's by a relative error of at most 0.001.
The roundings to bfloat16 on the way count: a program that leaves them out, or rounds other values in their place, can miss the bound.
Values may be sent and summed in bfloat16 or wider, within the bound.
No kernel may reach another device: no remote copies, remote signals or barrier semaphores. Data moves between devices by JAX's collectives and lax.ppermute only.
A program may use at most 64 MiB of HBM per device.

v0:
```python
import jax
import jax.numpy as jnp
from jax import lax
from jax.sharding import PartitionSpec as P

SNAPS = 3
STEPS = 3
LAG = 8


def extended(cells, sides, width):
    for axis, dim in sides:
        count = lax.axis_size(axis)
        ends = count - 1
        head = lax.slice_in_dim(cells, 0, width, axis=dim)
        tail = lax.slice_in_dim(cells, cells.shape[dim] - width, cells.shape[dim], axis=dim)
        cells = jnp.concatenate(
            [
                lax.ppermute(tail, axis, [(i, (i + 1) % count) for i in range(ends)]),
                cells,
                lax.ppermute(head, axis, [((i + 1) % count, i) for i in range(ends)]),
            ],
            axis=dim,
        )
    return cells


def coefficients(courant, epsilon, delta_param, tilt_angle):
    cos_tilt = jnp.cos(tilt_angle)
    sin_tilt = jnp.sin(tilt_angle)
    return (
        courant,
        1.0 + 2.0 * epsilon,
        1.0 + 2.0 * delta_param,
        cos_tilt * cos_tilt,
        sin_tilt * sin_tilt,
        2.0 * sin_tilt * cos_tilt,
    )


def second_diffs(padded):
    center = padded[..., 1:-1, 1:-1, 1:-1]
    along_z = padded[..., 2:, 1:-1, 1:-1] + padded[..., :-2, 1:-1, 1:-1] - 2.0 * center
    along_x = padded[..., 1:-1, 2:, 1:-1] + padded[..., 1:-1, :-2, 1:-1] - 2.0 * center
    along_y = padded[..., 1:-1, 1:-1, 2:] + padded[..., 1:-1, 1:-1, :-2] - 2.0 * center
    cross_xz = 0.25 * (
        padded[..., 2:, 2:, 1:-1]
        - padded[..., 2:, :-2, 1:-1]
        - padded[..., :-2, 2:, 1:-1]
        + padded[..., :-2, :-2, 1:-1]
    )
    return (along_z, along_x, along_y, cross_xz)


def advance(padded_p, padded_q, pressure, auxiliary, pressure_old, auxiliary_old, coeffs):
    courant, gain_eps, gain_delta, weight_z, weight_x, weight_mixed = coeffs
    p_zz, p_xx, p_yy, p_xz = second_diffs(padded_p)
    vert_p = weight_z * p_zz + weight_x * p_xx + weight_mixed * p_xz
    horiz_p = p_zz + p_xx + p_yy - vert_p
    q_zz, q_xx, _, q_xz = second_diffs(padded_q)
    vert_q = weight_z * q_zz + weight_x * q_xx + weight_mixed * q_xz
    new_p = 2.0 * pressure - pressure_old + courant * (gain_eps * horiz_p + vert_q)
    new_q = 2.0 * auxiliary - auxiliary_old + courant * (gain_delta * horiz_p + vert_q)
    return (new_p, new_q)


def deposit(field_3d, points, amounts, anchor, extent):
    local_pts = points - anchor[None, :]
    bounds = jnp.array(extent, jnp.int32)
    inside = jnp.all((local_pts >= 0) & (local_pts < bounds[None, :]), axis=1)
    clipped = jnp.clip(local_pts, 0, bounds[None, :] - 1)
    flat_index = (clipped[:, 0] * extent[1] + clipped[:, 1]) * extent[2] + clipped[:, 2]
    masked = jnp.where(inside, amounts, 0.0)
    return field_3d.reshape(-1).at[flat_index].add(masked).reshape(field_3d.shape)


def update(state, padded_p, padded_q, coeffs, points, amounts, anchor, extent, active):
    pressure, auxiliary, pressure_old, auxiliary_old = state
    new_p, new_q = advance(
        padded_p, padded_q, pressure, auxiliary, pressure_old, auxiliary_old, coeffs
    )
    new_p = deposit(new_p, points, amounts, anchor, extent)
    new_q = deposit(new_q, points, amounts, anchor, extent)
    return [
        jnp.where(active, new_p, pressure),
        jnp.where(active, new_q, auxiliary),
        jnp.where(active, pressure, pressure_old),
        jnp.where(active, auxiliary, auxiliary_old),
    ]


def lag_images(images, edges, offset_lags):
    depth_cells, wide_cells, side_cells = images.shape[1:]

    def one_lag(lag_pair):
        start_zero = jnp.zeros((), jnp.int32)
        source_win = lax.dynamic_slice(
            edges[0],
            (start_zero, LAG - lag_pair[0], LAG - lag_pair[1]),
            (depth_cells, wide_cells, side_cells),
        )
        receiver_win = lax.dynamic_slice(
            edges[1],
            (start_zero, LAG + lag_pair[0], LAG + lag_pair[1]),
            (depth_cells, wide_cells, side_cells),
        )
        return source_win.astype(jnp.float32) * receiver_win.astype(jnp.float32)

    return images + jax.vmap(one_lag)(offset_lags)


def snapshot_pair(source_p, receiver_p):
    stacked = jnp.stack([source_p, receiver_p]).astype(jnp.bfloat16)
    return extended(stacked, (("gx", 2), ("gy", 3)), LAG)


def local(
    source_fields,
    receiver_fields,
    courant,
    epsilon,
    delta_param,
    tilt_angle,
    source_pos,
    wavelet,
    receiver_pos,
    receiver_data,
    step_counts,
    offset_lags,
):
    depth_cells, wide_cells, side_cells = courant.shape
    anchor = jnp.stack(
        [
            lax.axis_index("sec") * depth_cells,
            lax.axis_index("gx") * wide_cells,
            lax.axis_index("gy") * side_cells,
        ]
    )
    positions = [source_pos.reshape(1, 3), receiver_pos]
    sections = [
        [source_fields[member] for member in range(4)],
        [receiver_fields[member] for member in range(4)],
    ]
    images = jnp.zeros((offset_lags.shape[0], depth_cells, wide_cells, side_cells), jnp.float32)
    coeffs = coefficients(courant, epsilon, delta_param, tilt_angle)
    extent = (depth_cells, wide_cells, side_cells)
    for snapshot in range(SNAPS):
        for substep in range(STEPS):
            time_slot = snapshot * STEPS + substep
            active = substep < step_counts[snapshot]
            amounts = [wavelet[time_slot].reshape(1), receiver_data[time_slot]]
            current = jnp.stack([sections[0][0], sections[0][1], sections[1][0], sections[1][1]])
            padded = extended(current, (("gx", 2), ("sec", 1), ("gy", 3)), 1)
            for section in range(2):
                sections[section] = update(
                    sections[section],
                    padded[2 * section],
                    padded[2 * section + 1],
                    coeffs,
                    positions[section],
                    amounts[section],
                    anchor,
                    extent,
                    active,
                )
        images = lag_images(images, snapshot_pair(sections[0][0], sections[1][0]), offset_lags)
    return (images.astype(jnp.bfloat16), jnp.stack(sections[0]), jnp.stack(sections[1]))


def solution(mesh):
    placed = (
        P("shot", "sec", "gx", "gy"),
        P("shot", "sec", "gx", "gy"),
        P("sec", "gx", "gy"),
        P("sec", "gx", "gy"),
        P("sec", "gx", "gy"),
        P("sec", "gx", "gy"),
        P("shot"),
        P("shot"),
        P("shot", None),
        P("shot", None),
        P(),
        P(),
    )
    return jax.shard_map(
        local,
        mesh=mesh,
        in_specs=placed,
        out_specs=(
            P("shot", "sec", "gx", "gy"),
            P("shot", "sec", "gx", "gy"),
            P("shot", "sec", "gx", "gy"),
        ),
        check_vma=False,
    )
```

profile of v0, /device:TPU:0, one launch (start us, length us, event | category | flops | bytes accessed | tf_op | source)
XLA Modules:
  0.0 927.1 jit_solution(13310554518553007526)
XLA Ops:
  2.3 5.0 collective-permute-start
  20.1 3.9 collective-permute-done.3
  38.3 4.5 collective-permute-start.6
  44.3 4.3 collective-permute-done.7
  51.9 4.2 collective-permute-done.9
  72.8 4.2 collective-permute-done.13
  80.3 4.2 collective-permute-done.15
  101.4 4.2 collective-permute-done.23
  108.9 4.2 collective-permute-done.25
  152.5 4.5 collective-permute-start.34
  162.7 4.6 collective-permute-start.36
  168.8 4.2 collective-permute-done.37
  186.0 4.0 collective-permute-start.44
  191.5 90.5 %while.24 = (s32[]{:T(128)}, bf16[8,24,144]{2,1,0:T(8,128)(2,1)S(1)}, s32[48,3]{0,1:T(4,128)S(1)}, bf16[48,8,8,128]{3,2,1,0:T(8,128)(2,1)S(1)}, s32[]{:T(128)}) while((s32[]{:T(128)}, bf16[8,24,144]{2,1,0:T(8,128)(2,1)S(1)}, s32[48,3]{0,1:T(4,128)S(1)}, bf16[48,8,8,128]{3,2,1,0:T(8,128)(2,1)S(1)}, s32[]{:T(128)}) %tuple.385), condition=%wide.while_cond.18, body=%wide.while_body.18.sunk | while | flops 2 | bytes 32885 | solution.py:97
  285.0 91.7 %while.25 = (s32[]{:T(128)}, bf16[8,24,144]{2,1,0:T(8,128)(2,1)S(1)}, s32[48,3]{0,1:T(4,128)S(1)}, bf16[48,8,8,128]{3,2,1,0:T(8,128)(2,1)S(1)}, s32[]{:T(128)}) while((s32[]{:T(128)}, bf16[8,24,144]{2,1,0:T(8,128)(2,1)S(1)}, s32[48,3]{0,1:T(4,128)S(1)}, bf16[48,8,8,128]{3,2,1,0:T(8,128)(2,1)S(1)}, s32[]{:T(128)}) %tuple.382), condition=%wide.while_cond.19, body=%wide.while_body.19.sunk | while | flops 2 | bytes 32885 | solution.py:102
  380.5 4.9 collective-permute-start.40
  395.4 4.5 collective-permute-start.50
  405.8 4.6 collective-permute-start.52
  434.1 4.2 collective-permute-done.57
  438.3 4.5 collective-permute-start.58
  444.3 102.2 %while.26 = (s32[]{:T(128)}, bf16[8,24,144]{2,1,0:T(8,128)(2,1)S(1)}, s32[48,3]{0,1:T(4,128)S(1)}, bf16[48,8,8,128]{3,2,1,0:T(8,128)(2,1)S(1)}, s32[]{:T(128)}) while((s32[]{:T(128)}, bf16[8,24,144]{2,1,0:T(8,128)(2,1)S(1)}, s32[48,3]{0,1:T(4,128)S(1)}, bf16[48,8,8,128]{3,2,1,0:T(8,128)(2,1)S(1)}, s32[]{:T(128)}) %tuple.390), condition=%wide.while_cond.20, body=%wide.while_body.20.sunk | while | flops 2 | bytes 32885 | solution.py:97
  552.0 126.2 %while.27 = (s32[]{:T(128)}, bf16[8,24,144]{2,1,0:T(8,128)(2,1)S(1)}, s32[48,3]{0,1:T(4,128)S(1)}, bf16[48,8,8,128]{3,2,1,0:T(8,128)(2,1)}, s32[]{:T(128)}) while((s32[]{:T(128)}, bf16[8,24,144]{2,1,0:T(8,128)(2,1)S(1)}, s32[48,3]{0,1:T(4,128)S(1)}, bf16[48,8,8,128]{3,2,1,0:T(8,128)(2,1)}, s32[]{:T(128)}) %tuple.388), condition=%wide.while_cond.21, body=%wide.while_body.21.sunk | while | flops 2 | bytes 34409 | solution.py:102
  700.1 131.3 %while.28 = (s32[]{:T(128)}, bf16[8,24,144]{2,1,0:T(8,128)(2,1)S(1)}, s32[48,3]{0,1:T(4,128)S(1)}, bf16[48,8,8,128]{3,2,1,0:T(8,128)(2,1)}, s32[]{:T(128)}) while((s32[]{:T(128)}, bf16[8,24,144]{2,1,0:T(8,128)(2,1)S(1)}, s32[48,3]{0,1:T(4,128)S(1)}, bf16[48,8,8,128]{3,2,1,0:T(8,128)(2,1)}, s32[]{:T(128)}) %tuple.391), condition=%wide.while_cond.22, body=%wide.while_body.22.sunk | while | flops 2 | bytes 34409 | solution.py:97
  831.7 92.0 %while.29 = (s32[]{:T(128)}, bf16[8,24,144]{2,1,0:T(8,128)(2,1)S(1)}, s32[48,3]{0,1:T(4,128)S(1)}, bf16[48,8,8,128]{3,2,1,0:T(8,128)(2,1)S(1)}, s32[]{:T(128)}) while((s32[]{:T(128)}, bf16[8,24,144]{2,1,0:T(8,128)(2,1)S(1)}, s32[48,3]{0,1:T(4,128)S(1)}, bf16[48,8,8,128]{3,2,1,0:T(8,128)(2,1)S(1)}, s32[]{:T(128)}) %tuple.389), condition=%wide.while_cond.23, body=%wide.while_body.23.sunk | while | flops 2 | bytes 32885 | solution.py:102
  (1261 shorter events, 834.3 us)
Async XLA Ops:
  2.3 12.5 %collective-permute-start = (f32[4,8,1,128]{3,2,1,0:T(1,128)S(1)}, f32[4,8,1,128]{3,2,1,0:T(1,128)S(1)}, u32[]{:S(2)}, u32[]{:S(2)}) collective-permute-start(f32[4,8,1,128]{3,2,1,0:T(1,128)S(1)} %get-tuple-element.554), channel_id=1, source_target_pairs={{0,4},{4,8},{8,12},{1,5},{5,9},{9,13},{2,6},{6,10},{10,14},{3,7},{... | collective-permute-start | bytes 49160 | tf_op jit(solution)/shard_map/ppermute | solution.py:19
  7.3 7.5 collective-permute-start.1
  24.3 6.4 collective-permute-start.4
  124.9 6.3 collective-permute-start.28
  132.5 7.6 collective-permute-start.30
  135.5 7.5 collective-permute-start.18
  152.5 9.0 collective-permute-start.34
  158.4 10.1 %collective-permute-start.20 = (bf16[2,8,24,8]{3,2,1,0:T(8,128)(2,1)S(1)}, bf16[2,8,24,8]{3,2,1,0:T(8,128)(2,1)S(1)}, u32[]{:S(2)}, u32[]{:S(2)}) collective-permute-start(bf16[2,8,24,8]{3,2,1,0:T(8,128)(2,1)S(1)} %get-tuple-element.556), channel_id=1, source_target_pairs={{0,1},{2,3},{4,5},{6,7},{8,9},{10,11},{12,13},{14,15},{16,17},{18,... | collective-permute-start | bytes 18440 | tf_op jit(solution)/shard_map/ppermute | solution.py:19
  160.2 8.4 collective-permute-start.21
  186.0 96.0 %collective-permute-start.44 = (f32[4,8,1,128]{3,2,1,0:T(1,128)S(1)}, f32[4,8,1,128]{3,2,1,0:T(1,128)S(1)}, u32[]{:S(2)}, u32[]{:S(2)}) collective-permute-start(f32[4,8,1,128]{3,2,1,0:T(1,128)S(1)} %get-tuple-element.538), channel_id=1, source_target_pairs={{0,4},{4,8},{8,12},{1,5},{5,9},{9,13},{2,6},{6,10},{10,14},{3,7},{... | collective-permute-start | bytes 49160 | tf_op jit(solution)/shard_map/ppermute | solution.py:19
  190.0 92.0 %collective-permute-start.45 = (f32[4,8,1,128]{3,2,1,0:T(1,128)S(1)}, f32[4,8,1,128]{3,2,1,0:T(1,128)S(1)}, u32[]{:S(2)}, u32[]{:S(2)}) collective-permute-start(f32[4,8,1,128]{3,2,1,0:T(1,128)S(1)} %get-tuple-element.539), channel_id=1, source_target_pairs={{4,0},{8,4},{12,8},{5,1},{9,5},{13,9},{6,2},{10,6},{14,10},{7,3},{... | collective-permute-start | bytes 49160 | tf_op jit(solution)/shard_map/ppermute | solution.py:21
  282.1 94.7 %collective-permute-start.46 = (f32[4,1,10,128]{3,2,1,0:T(8,128)S(1)}, f32[4,1,10,128]{3,2,1,0:T(8,128)S(1)}, u32[]{:S(2)}, u32[]{:S(2)}) collective-permute-start(f32[4,1,10,128]{3,2,1,0:T(8,128)S(1)} %get-tuple-element.520), channel_id=1, source_target_pairs={{0,2},{1,3},{4,6},{5,7},{8,10},{9,11},{12,14},{13,15},{16,18},{17,... | collective-permute-start | bytes 61448 | tf_op jit(solution)/shard_map/ppermute | solution.py:19
  283.6 93.2 %collective-permute-start.47 = (f32[4,1,10,128]{3,2,1,0:T(8,128)S(1)}, f32[4,1,10,128]{3,2,1,0:T(8,128)S(1)}, u32[]{:S(2)}, u32[]{:S(2)}) collective-permute-start(f32[4,1,10,128]{3,2,1,0:T(8,128)S(1)} %get-tuple-element.521), channel_id=1, source_target_pairs={{2,0},{3,1},{6,4},{7,5},{10,8},{11,9},{14,12},{15,13},{18,16},{19,... | collective-permute-start | bytes 61448 | tf_op jit(solution)/shard_map/ppermute | solution.py:21
  377.0 9.7 %collective-permute-start.48 = (f32[4,10,10,1]{3,2,1,0:T(8,128)S(1)}, f32[4,10,10,1]{3,2,1,0:T(8,128)S(1)}, u32[]{:S(2)}, u32[]{:S(2)}) collective-permute-start(f32[4,10,10,1]{3,2,1,0:T(8,128)S(1)} %get-tuple-element.496), channel_id=1, source_target_pairs={{0,1},{2,3},{4,5},{6,7},{8,9},{10,11},{12,13},{14,15},{16,17},{18,... | collective-permute-start | bytes 4808 | tf_op jit(solution)/shard_map/ppermute | solution.py:19
  378.6 8.1 collective-permute-start.49
  380.5 20.9 %collective-permute-start.40 = (bf16[2,8,8,128]{3,2,1,0:T(8,128)(2,1)}, bf16[2,8,8,128]{3,2,1,0:T(8,128)(2,1)}, u32[]{:S(2)}, u32[]{:S(2)}) collective-permute-start(bf16[2,8,8,128]{3,2,1,0:T(8,128)(2,1)} %pad_maximum_fusion.79), channel_id=1, source_target_pairs={{0,4},{4,8},{8,12},{1,5},{5,9},{9,13},{2,6},{6,10},{10,14},{3,7},{... | collective-permute-start | bytes 98312 | tf_op jit(solution)/shard_map/ppermute | solution.py:19
  385.4 16.1 %collective-permute-start.41 = (bf16[2,8,8,128]{3,2,1,0:T(8,128)(2,1)}, bf16[2,8,8,128]{3,2,1,0:T(8,128)(2,1)}, u32[]{:S(2)}, u32[]{:S(2)}) collective-permute-start(bf16[2,8,8,128]{3,2,1,0:T(8,128)(2,1)} %pad_maximum_fusion.79), channel_id=1, source_target_pairs={{4,0},{8,4},{12,8},{5,1},{9,5},{13,9},{6,2},{10,6},{14,10},{7,3},{... | collective-permute-start | bytes 98312 | tf_op jit(solution)/shard_map/ppermute | solution.py:21
  395.4 6.9 collective-permute-start.50
  405.8 8.6 collective-permute-start.52
  411.8 7.3 collective-permute-start.42
  438.3 108.3 %collective-permute-start.58 = (f32[4,1,10,128]{3,2,1,0:T(8,128)S(1)}, f32[4,1,10,128]{3,2,1,0:T(8,128)S(1)}, u32[]{:S(2)}, u32[]{:S(2)}) collective-permute-start(f32[4,1,10,128]{3,2,1,0:T(8,128)S(1)} %get-tuple-element.516), channel_id=1, source_target_pairs={{0,2},{1,3},{4,6},{5,7},{8,10},{9,11},{12,14},{13,15},{16,18},{17,... | collective-permute-start | bytes 61448 | tf_op jit(solution)/shard_map/ppermute | solution.py:19
  442.9 103.7 %collective-permute-start.59 = (f32[4,1,10,128]{3,2,1,0:T(8,128)S(1)}, f32[4,1,10,128]{3,2,1,0:T(8,128)S(1)}, u32[]{:S(2)}, u32[]{:S(2)}) collective-permute-start(f32[4,1,10,128]{3,2,1,0:T(8,128)S(1)} %get-tuple-element.517), channel_id=1, source_target_pairs={{2,0},{3,1},{6,4},{7,5},{10,8},{11,9},{14,12},{15,13},{18,16},{19,... | collective-permute-start | bytes 61448 | tf_op jit(solution)/shard_map/ppermute | solution.py:21
  547.6 130.5 %collective-permute-start.60 = (f32[4,10,10,1]{3,2,1,0:T(8,128)}, f32[4,10,10,1]{3,2,1,0:T(8,128)}, u32[]{:S(2)}, u32[]{:S(2)}) collective-permute-start(f32[4,10,10,1]{3,2,1,0:T(8,128)} %get-tuple-element.492), channel_id=1, source_target_pairs={{0,1},{2,3},{4,5},{6,7},{8,9},{10,11},{12,13},{14,15},{16,17},{18,... | collective-permute-start | bytes 4808 | tf_op jit(solution)/shard_map/ppermute | solution.py:19
  549.6 128.5 %collective-permute-start.61 = (f32[4,10,10,1]{3,2,1,0:T(8,128)}, f32[4,10,10,1]{3,2,1,0:T(8,128)}, u32[]{:S(2)}, u32[]{:S(2)}) collective-permute-start(f32[4,10,10,1]{3,2,1,0:T(8,128)} %get-tuple-element.493), channel_id=1, source_target_pairs={{1,0},{3,2},{5,4},{7,6},{9,8},{11,10},{13,12},{15,14},{17,16},{19,... | collective-permute-start | bytes 4808 | tf_op jit(solution)/shard_map/ppermute | solution.py:21
  (93 other events, 1093.7 us)
where the time goes:
time: 945 us; the launch traced here: 927 us
  local copies, waits for them, and re-layouts  645 us (68%)
  starting transfers between devices  130 us (14%)
  other arithmetic  78.1 us (8%)
  waiting for transfers between devices  60.2 us (6%)
  between operations  10.6 us (1%)
    gather x864, local copies, waits for them, and re-layouts  631 us
    ppermute x33, starting transfers between devices, extended(): lax.ppermute(tail, axis, [(i, (i + 1) % count) for i in range(ends)])  87.1 us
    ppermute x33, waiting for transfers between devices, extended(): lax.ppermute(head, axis, [((i + 1) % count, i) for i in range(ends)])  58.7 us
    scatter-add x27, other arithmetic, deposit(): field_3d.reshape(-1).at[flat_index].add(masked).reshape(field_3d.shape)  50.8 us
    ppermute x33, starting transfers between devices, extended(): lax.ppermute(head, axis, [((i + 1) % count, i) for i in range(ends)])  42.8 us
  transfers between devices with their start and end apart: 66, of which 30 were waited for; matrix products, arithmetic and copies ran while one was open for 47% of the time, Pallas kernels for 0%

commit v1 on v0

v1 whole, which is shorter than its diff:
```python
import functools

import jax
import jax.numpy as jnp
from jax import lax
from jax.experimental import pallas as pl
from jax.experimental.pallas import tpu as pltpu
from jax.sharding import PartitionSpec as P

SNAPS = 3
STEPS = 3
LAG = 8
HALO = 4
ROWS = 4
WROWS = ROWS + 2 * HALO
ZB = 8
WZ = ZB + 2 * HALO
LANES = 128

F32 = jnp.float32
BF16 = jnp.bfloat16
VM = pl.BlockSpec(memory_space=pltpu.VMEM)
SM = pl.BlockSpec(memory_space=pltpu.SMEM)


def call(body, outs, n_smem, n_vmem, scratch=(), flops=100000, moved=1000000):
    return pl.pallas_call(
        body,
        out_shape=outs,
        in_specs=[SM] * n_smem + [VM] * n_vmem,
        out_specs=[VM] * len(outs),
        scratch_shapes=list(scratch),
        cost_estimate=pl.CostEstimate(flops=flops, bytes_accessed=moved, transcendentals=0),
    )


def half_swap(value):
    return pltpu.roll(value, HALO, 0)


def low_sublanes(shape):
    return lax.broadcasted_iota(jnp.int32, shape, 0) < HALO


def split_body(src, rec, courant, epsilon, delta, tilt, keep, send):
    low = lax.axis_index("gy") == 0

    def put(slot, pick, change=lambda v: v):
        for r in range(ROWS):
            lo = change(pick(pl.ds(r, ZB, stride=2 * ROWS)))
            hi = change(pick(pl.ds(r + ROWS, ZB, stride=2 * ROWS)))
            keep[slot, r] = jnp.where(low, lo, hi)
            send[slot, r] = jnp.where(low, hi, lo)

    for member in range(4):
        put(member, lambda s, m=member: src[m, s, :])
        put(4 + member, lambda s, m=member: rec[m, s, :])
    put(8, lambda s: courant[s, :])
    put(9, lambda s: epsilon[s, :])
    put(10, lambda s: delta[s, :])
    put(11, lambda s: tilt[s, :], jnp.sin)


def edges_of(first, second, sec_size):
    sub = low_sublanes(first.shape)
    top = jnp.where(sub, half_swap(first), second)
    bottom = jnp.where(sub, first, half_swap(second))
    if sec_size == 2:
        return [jnp.where(lax.axis_index("sec") == 0, top, bottom)]
    return [top, bottom]


def merge_body(sec_size, keep, got, own, *edges):
    low = lax.axis_index("gy") == 0

    def pair(j, _):
        for r in range(ROWS):
            both = []
            for k in range(2):
                a, b = keep[2 * j + k, r], got[2 * j + k, r]
                whole = jnp.concatenate([jnp.where(low, a, b), jnp.where(low, b, a)], axis=1)
                own[2 * j + k, r] = whole
                both.append(whole)
            for ref, edge in zip(edges, edges_of(both[0], both[1], sec_size)):
                ref[j, r] = edge
        return 0

    lax.fori_loop(0, 6, pair, 0)


def inject_body(pos, pos_t, data, out):
    x0 = lax.axis_index("gx") * (2 * ROWS) + lax.axis_index("gy") * ROWS - HALO
    z0 = lax.axis_index("sec") * ZB - HALO
    count, side = pos.shape[0], out.shape[3]
    slots = out.shape[0]
    zw = pos_t[0:1, :] - z0
    xw = pos_t[1:2, :] - x0
    inside = (zw >= 0) & (zw < WZ) & (xw >= 0) & (xw < WROWS)
    cell = jnp.where(inside, xw * WZ + zw, -1)
    hit = lax.broadcasted_iota(jnp.int32, (WROWS * WZ, count), 0) == cell
    lanes = lax.broadcasted_iota(jnp.int32, (count, side), 1)
    onehot = jnp.where(lanes == pos[:, 2:3], 1.0, 0.0).astype(BF16)

    for t in range(slots):
        amount = data[t : t + 1, :]
        first = amount.astype(BF16).astype(F32)
        rest = amount - first
        second = rest.astype(BF16).astype(F32)
        third = rest - second
        total = None
        for part in (first, second, third):
            left = jnp.where(hit, part, 0.0).astype(BF16)
            term = jnp.dot(left, onehot, preferred_element_type=F32)
            total = term if total is None else total + term
        out[t] = total.reshape(WROWS, WZ, side)


def assemble(dest, j, base, own, halos, sec_size, slot):
    sec = lax.axis_index("sec")
    for r in range(ROWS):
        sub = low_sublanes(own.shape[2:])
        below = halos[0][j, r]
        if sec_size == 2:
            zero = jnp.zeros_like(below)
            above = jnp.where(sec == 0, below, zero)
            below = jnp.where(sec > 0, below, zero)
        else:
            above = halos[1][j, r]
        lows = (below, half_swap(below))
        highs = (half_swap(above), above)
        for k in range(2):
            mid = half_swap(own[2 * j + k, r])
            ref = dest(slot, k)
            ref[base + r, 0:ZB, :] = jnp.where(sub, lows[k], mid)
            ref[base + r, ZB:WZ, :] = jnp.where(sub, mid, highs[k])


def round_body(number, sec_size, has_snaps, more, last, *refs):
    refs = list(refs)

    def take(n):
        out = refs[:n]
        del refs[:n]
        return out

    nz = 1 if sec_size == 2 else 2
    counts, wavelet, source_pos = take(3)
    groups = []
    for _ in range(3):
        groups.append((take(1)[0], take(nz)))
    coef_groups = []
    for _ in range(3):
        coef_groups.append((take(1)[0], take(nz)))
    inject = take(1)[0]
    snaps_in = take(1)[0] if has_snaps else None
    own_out, snaps = take(2)
    edge_outs = take(nz) if more else []
    final_send = take(1)[0] if last else None
    work, coef, raw = take(3)

    low = lax.axis_index("gy") == 0
    sec = lax.axis_index("sec")
    zero = jnp.int32(0)
    bases = [
        jnp.int32(HALO),
        jnp.where(low, HALO + ROWS, 0),
        jnp.where(low, 0, HALO + ROWS),
    ]

    def fields(j, _):
        for base, (own, halos) in zip(bases, groups):
            assemble(
                lambda slot, k: work.at[j % 2, j // 2, k], j, base, own, halos, sec_size, None
            )
        return 0

    lax.fori_loop(0, 4, fields, 0)

    for j in range(2):
        for base, (own, halos) in zip(bases, coef_groups):
            assemble(lambda slot, k: raw.at[2 * j + k], j, base, own, halos, sec_size, None)

    def derive(x, _):
        c = raw[0, x]
        s = raw[3, x]
        wx = s * s
        wz = 1.0 - wx
        coef[0, x] = c
        coef[1, x] = c * (1.0 + 2.0 * raw[1, x])
        coef[2, x] = c * (1.0 + 2.0 * raw[2, x])
        coef[3, x] = wz
        coef[4, x] = wx
        coef[5, x] = 0.5 * s * jnp.sqrt(wz)
        return 0

    lax.fori_loop(1, WROWS - 1, derive, 0)

    if has_snaps:
        snaps[...] = snaps_in[...]

    ends = []
    total = zero
    for s in range(SNAPS):
        total = total + counts[s]
        ends.append(total)
    first = number * HALO
    todo = jnp.clip(total - first, 0, HALO)
    side = work.shape[-1]
    tile = (WZ, side)
    lane = lax.broadcasted_iota(jnp.int32, tile, 1)
    depth = lax.broadcasted_iota(jnp.int32, tile, 0)
    x0 = lax.axis_index("gx") * (2 * ROWS) + lax.axis_index("gy") * ROWS - HALO
    sx = source_pos[1] - x0
    sz = source_pos[0] - (sec * ZB - HALO)
    sy = source_pos[2]

    def own_cells(parity, section, which, r):
        value = work[parity, section, which, HALO + r]
        sub = low_sublanes((ZB, side))
        return jnp.where(sub, half_swap(value[0:ZB]), half_swap(value[ZB:WZ]))

    def step(j, _):
        active = first + j
        slot = zero
        start = zero
        for s in range(SNAPS):
            slot = jnp.where(active >= start, s * STEPS + active - start, slot)
            start = ends[s]
        cur = j % 2
        new = 1 - cur
        margin = todo - 1 - j

        def row(x, _):
            c, ce, cd, wz, wx, wm = (coef[i, x] for i in range(6))
            for section in range(2):
                p = work[cur, section, 0, x]
                pm = work[cur, section, 0, x - 1]
                pp = work[cur, section, 0, x + 1]
                p2 = 2.0 * p
                diff = pp - pm
                dzz = pltpu.roll(p, 1, 0) + pltpu.roll(p, WZ - 1, 0) - p2
                dxx = pp + pm - p2
                dxz = pltpu.roll(diff, WZ - 1, 0) - pltpu.roll(diff, 1, 0)
                left = jnp.where(lane > 0, pltpu.roll(p, 1, 1), 0.0)
                right = jnp.where(lane < side - 1, pltpu.roll(p, side - 1, 1), 0.0)
                dyy = left + right - p2
                vert = wz * dzz + wx * dxx + wm * dxz
                horiz = dzz + dxx + dyy - vert
                q = work[cur, section, 1, x]
                qm = work[cur, section, 1, x - 1]
                qp = work[cur, section, 1, x + 1]
                q2 = 2.0 * q
                qdiff = qp - qm
                qzz = pltpu.roll(q, 1, 0) + pltpu.roll(q, WZ - 1, 0) - q2
                qxx = qp + qm - q2
                qxz = pltpu.roll(qdiff, WZ - 1, 0) - pltpu.roll(qdiff, 1, 0)
                vq = c * (wz * qzz + wx * qxx + wm * qxz)
                np_ = p2 - work[new, section, 0, x] + (ce * horiz + vq)
                nq_ = q2 - work[new, section, 1, x] + (cd * horiz + vq)
                if section == 1:
                    extra = inject[slot, x]
                    np_ = np_ + extra
                    nq_ = nq_ + extra
                work[new, section, 0, x] = np_
                work[new, section, 1, x] = nq_
            return 0

        lax.fori_loop(HALO - margin, HALO + ROWS + margin, row, 0)

        @pl.when((sx >= 0) & (sx < WROWS))
        def _():
            here = jnp.where((depth == sz) & (lane == sy), wavelet[slot], 0.0)
            for which in range(2):
                work[new, 0, which, sx] = work[new, 0, which, sx] + here

        for s in range(SNAPS):

            @pl.when(active + 1 == ends[s])
            def _():
                for r in range(ROWS):
                    both = [own_cells(new, section, 0, r) for section in range(2)]
                    snaps[s, r] = jnp.concatenate(both, axis=0).astype(BF16)

        return 0

    lax.fori_loop(0, todo, step, 0)

    at = todo % 2
    for section in range(2):
        for old in range(2):
            parity = at if old == 0 else 1 - at
            for r in range(ROWS):
                both = []
                for which in range(2):
                    value = own_cells(parity, section, which, r)
                    member = section * 4 + old * 2 + which
                    own_out[member, r] = value
                    if last:
                        final_send[member, r] = jnp.where(
                            low, value[:, side // 2 :], value[:, : side // 2]
                        )
                    both.append(value)
                if more:
                    for ref, edge in zip(edge_outs, edges_of(both[0], both[1], sec_size)):
                        ref[section * 2 + old, r] = edge


def image_body(lags, own, got, snaps, sib, near, far, sib_near, sib_far, images, src, rec, ext, flip):
    core = lax.axis_index("gy")
    low = core == 0
    half = images.shape[3]
    mine = jnp.where(low, 0, ROWS)
    other = jnp.where(low, ROWS, 0)
    for member in range(8):
        dest = src if member < 4 else rec
        base = (member % 4) * ZB * 2 * ROWS
        for r in range(ROWS):
            value = own[member, r]
            value = jnp.where(low, value[:, :half], value[:, half:])
            dest[pl.ds(base + mine + r, ZB, stride=2 * ROWS), :] = value
            dest[pl.ds(base + other + r, ZB, stride=2 * ROWS), :] = got[member, r]

    lane = lax.broadcasted_iota(jnp.int32, (ZB, half), 1)
    edge = jnp.where(low, 0, half - LAG)
    keep = (lane >= edge) & (lane < edge + LAG)
    pieces = (
        (near, jnp.where(low, ROWS, 4 * ROWS)),
        (far, jnp.where(low, 0, 5 * ROWS)),
        (snaps, jnp.where(low, 2 * ROWS, 3 * ROWS)),
        (sib, jnp.where(low, 3 * ROWS, 2 * ROWS)),
        (sib_near, jnp.where(low, 4 * ROWS, ROWS)),
        (sib_far, jnp.where(low, 5 * ROWS, 0)),
    )
    for piece, base in pieces:
        for s in range(SNAPS):
            for r in range(ROWS):
                value = piece[s, r].astype(F32)
                for section in range(2):
                    cells = value[section * ZB : (section + 1) * ZB]
                    a, b = cells[:, :half], cells[:, half:]
                    ext[s, section, base + r, 0] = jnp.where(low, a, b)
                    ext[s, section, base + r, 1] = jnp.where(keep, jnp.where(low, b, a), 0.0)

    def one_lag(l, _):
        lx = lags[l, 0]
        ly = lags[l, 1]
        s_shift = lax.rem(ly + half, half)
        r_shift = lax.rem(half - ly, half)
        s_own = (lane - ly >= 0) & (lane - ly < half)
        r_own = (lane + ly >= 0) & (lane + ly < half)
        for x in range(2 * ROWS):
            total = None
            for s in range(SNAPS):
                xs = 2 * ROWS + x - lx
                xr = 2 * ROWS + x + lx
                a = jnp.where(
                    s_own,
                    pltpu.roll(ext[s, 0, xs, 0], s_shift, 1),
                    pltpu.roll(ext[s, 0, xs, 1], s_shift, 1),
                )
                b = jnp.where(
                    r_own,
                    pltpu.roll(ext[s, 1, xr, 0], r_shift, 1),
                    pltpu.roll(ext[s, 1, xr, 1], r_shift, 1),
                )
                total = a * b if total is None else total + a * b
            flip[pl.ds(x, ZB, stride=2 * ROWS), :] = total
        for z in range(ZB):
            images[l, z] = flip[z * 2 * ROWS : (z + 1) * 2 * ROWS, :].astype(BF16)
        return 0

    lax.fori_loop(0, lags.shape[0], one_lag, 0)


def local(
    source_fields,
    receiver_fields,
    courant,
    epsilon,
    delta_param,
    tilt_angle,
    source_pos,
    wavelet,
    receiver_pos,
    receiver_data,
    step_counts,
    offset_lags,
):
    sec_size = lax.axis_size("sec")
    gx_size = lax.axis_size("gx")
    depth_cells, wide_cells, half = courant.shape
    side = 2 * half
    sib_pairs = [(0, 1), (1, 0)]
    partner_pairs = []
    for i in range(gx_size - 1):
        partner_pairs += [(2 * i + 1, 2 * i + 2), (2 * i + 2, 2 * i + 1)]

    def sibling(x):
        return lax.ppermute(x, "gy", sib_pairs)

    def partner(x):
        return lax.ppermute(x, ("gx", "gy"), partner_pairs)

    def depth_halos(edges):
        if sec_size == 2:
            return [lax.ppermute(edges[0], "sec", sib_pairs)]
        up = [(i, i + 1) for i in range(sec_size - 1)]
        down = [(i + 1, i) for i in range(sec_size - 1)]
        return [lax.ppermute(edges[0], "sec", up), lax.ppermute(edges[1], "sec", down)]

    def flat(x):
        return x.reshape(x.shape[:-3] + (depth_cells * wide_cells, half))

    part = jax.ShapeDtypeStruct((12, ROWS, ZB, half), F32)
    keep, send = call(split_body, [part, part], 0, 6)(
        flat(source_fields),
        flat(receiver_fields),
        flat(courant),
        flat(epsilon),
        flat(delta_param),
        flat(tilt_angle),
    )
    got = sibling(send)
    nz = 1 if sec_size == 2 else 2
    edge12 = jax.ShapeDtypeStruct((6, ROWS, ZB, side), F32)
    edge8 = jax.ShapeDtypeStruct((4, ROWS, ZB, side), F32)
    merged = call(
        functools.partial(merge_body, sec_size),
        [jax.ShapeDtypeStruct((12, ROWS, ZB, side), F32)] + [edge12] * nz,
        0,
        2,
    )(keep, got)
    own, edges = merged[0], merged[1:]

    slots = receiver_data.shape[0]
    (inject,) = call(
        inject_body, [jax.ShapeDtypeStruct((slots, WROWS, WZ, side), F32)], 0, 3
    )(receiver_pos, receiver_pos.T, receiver_data)

    def exchange(own, edges):
        sib_own, par_own = sibling(own), partner(own)
        halos = depth_halos(edges)
        groups = [(own, halos)]
        groups.append((sib_own, [sibling(h) for h in halos]))
        groups.append((par_own, [partner(h) for h in halos]))
        return groups

    snap_type = jax.ShapeDtypeStruct((SNAPS, ROWS, 2 * ZB, side), BF16)
    own_type = jax.ShapeDtypeStruct((8, ROWS, ZB, side), F32)
    fin_type = jax.ShapeDtypeStruct((8, ROWS, ZB, half), F32)

    def whole_or_part(shape, first, count):
        return pl.BlockSpec((count,) + shape[1:], lambda i, b=first // count: (b, 0, 0, 0))

    def run_round(number, groups, coef_groups, snaps, more, last):
        args, specs = [step_counts, wavelet, source_pos], [SM] * 3
        for own_, halos in groups:
            args.append(own_)
            specs.append(whole_or_part(own_.shape, 0, 8) if own_.shape[0] == 8 else pl.BlockSpec((8,) + own_.shape[1:], lambda i: (0, 0, 0, 0)))
            for h in halos:
                args.append(h)
                specs.append(pl.BlockSpec((4,) + h.shape[1:], lambda i: (0, 0, 0, 0)))
        for own_, halos in coef_groups:
            args.append(own_)
            specs.append(pl.BlockSpec((4,) + own_.shape[1:], lambda i: (2, 0, 0, 0)))
            for h in halos:
                args.append(h)
                specs.append(pl.BlockSpec((2,) + h.shape[1:], lambda i: (2, 0, 0, 0)))
        args.append(inject)
        specs.append(VM)
        if snaps is not None:
            args.append(snaps)
            specs.append(VM)
        outs = [own_type, snap_type]
        if more:
            outs += [edge8] * nz
        if last:
            outs += [fin_type]
        return pl.pallas_call(
            functools.partial(round_body, number, sec_size, snaps is not None, more, last),
            out_shape=outs,
            grid=(1,),
            in_specs=specs,
            out_specs=[VM] * len(outs),
            scratch_shapes=[
                pltpu.VMEM((2, 2, 2, WROWS, WZ, side), F32),
                pltpu.VMEM((6, WROWS, WZ, side), F32),
                pltpu.VMEM((4, WROWS, WZ, side), F32),
            ],
            cost_estimate=pl.CostEstimate(flops=10000000, bytes_accessed=3000000, transcendentals=0),
        )(*args)

    groups0 = exchange(own, edges)
    own, snaps, *edges = run_round(0, groups0, groups0, None, True, False)
    groups = exchange(own, edges)
    own, snaps, *rest = run_round(1, groups, groups0, snaps, True, True)
    edges, final_send = rest[:nz], rest[nz]

    def finish(own, snaps, final_send):
        final_got = sibling(final_send)
        sib = sibling(snaps)
        near, far = partner(snaps), partner(sib)
        sib_near, sib_far = sibling(near), sibling(far)
        n_lags = offset_lags.shape[0]
        out = jax.ShapeDtypeStruct((4 * depth_cells * wide_cells, half), F32)
        images, src, rec = call(
            image_body,
            [jax.ShapeDtypeStruct((n_lags, depth_cells, wide_cells, half), BF16), out, out],
            1,
            8,
            [
                pltpu.VMEM((SNAPS, 2, 6 * ROWS, 2, ZB, half), F32),
                pltpu.VMEM((ZB * 2 * ROWS, half), F32),
            ],
        )(offset_lags, own, final_got, snaps, sib, near, far, sib_near, sib_far)
        shape = (4, depth_cells, wide_cells, half)
        return images, src.reshape(shape), rec.reshape(shape)

    def third(own, snaps, final_send, *edges):
        groups = exchange(own, list(edges))
        own, snaps, final_send = run_round(2, groups, groups0, snaps, False, True)
        return finish(own, snaps, final_send)

    def done(own, snaps, final_send, *edges):
        return finish(own, snaps, final_send)

    return lax.cond(
        jnp.sum(step_counts) > 2 * HALO, third, done, own, snaps, final_send, *edges
    )


def solution(mesh):
    placed = (
        P("shot", "sec", "gx", "gy"),
        P("shot", "sec", "gx", "gy"),
        P("sec", "gx", "gy"),
        P("sec", "gx", "gy"),
        P("sec", "gx", "gy"),
        P("sec", "gx", "gy"),
        P("shot"),
        P("shot"),
        P("shot", None),
        P("shot", None),
        P(),
        P(),
    )
    return jax.shard_map(
        local,
        mesh=mesh,
        in_specs=placed,
        out_specs=(
            P("shot", "sec", "gx", "gy"),
            P("shot", "sec", "gx", "gy"),
            P("shot", "sec", "gx", "gy"),
        ),
        check_vma=False,
    )
```

time: 945 us -> 72.9 us (0.08); the launches traced: 927 us -> 72.4 us
  local copies, waits for them, and re-layouts: 645 us -> 7.4 us
  starting transfers between devices: 130 us -> 30.6 us
  other arithmetic: 78.1 us -> 0.63 us
  waiting for transfers between devices: 60.2 us -> 4.4 us
  Pallas kernels: 0 us -> 27.9 us
    gather x864 -> x0, local copies, waits for them, and re-layouts: 631 us -> none
    ppermute x66 -> x17, starting transfers between devices: 130 us -> 30.6 us  [the longest x9 21 us: sibling(): return lax.ppermute(x, 'gy', sib_pairs)]
    ppermute x66 -> x17, waiting for transfers between devices: 60.2 us -> 4.4 us  [the longest x2 2.33 us: depth_halos(): return [lax.ppermute(edges[0], 'sec', sib_pairs)]]
    scatter-add x27 -> x0, other arithmetic: 50.8 us -> none  [deposit(): field_3d.reshape(-1).at[flat_index].add(masked).reshape(field_3d.shape)]
    pallas_call x0 -> x6, Pallas kernels: none -> 27.9 us  [the longest x2 11.2 us: run_round(): pl.pallas_call(functools.partial(round_body, number, sec_size, snaps is n...]
  transfers between devices with their start and end apart: 66 -> 17, of which waited for: 30 -> 5; matrix products, arithmetic and copies ran while one was open for 47% -> 4% of each run, Pallas kernels for 0% -> 3%
where the time goes in v1:
time: 72.9 us; the launch traced here: 72.4 us
  starting transfers between devices  30.6 us (42%)
  Pallas kernels  27.9 us (38%)
  local copies, waits for them, and re-layouts  7.4 us (10%)
  waiting for transfers between devices  4.4 us (6%)
  between operations  1.42 us (2%)
    ppermute x9, starting transfers between devices, sibling(): return lax.ppermute(x, 'gy', sib_pairs)  21 us
    pallas_call x2, Pallas kernels, run_round(): pl.pallas_call(functools.partial(round_body, number, sec_size, snaps is n...  11.2 us
    pallas_call x1, Pallas kernels, finish(): call(image_body, [jax.ShapeDtypeStruct((n_lags, depth_cells, wide_cells,...  11.1 us
    ppermute x6, starting transfers between devices, partner(): return lax.ppermute(x, ('gx', 'gy'), partner_pairs)  5.32 us
    ppermute x2, starting transfers between devices, depth_halos(): return [lax.ppermute(edges[0], 'sec', sib_pairs)]  4.34 us
    cond x15, local copies, waits for them, and re-layouts  3.59 us
    unnamed x17, local copies, waits for them, and re-layouts  3.13 us
    ppermute x2, waiting for transfers between devices, depth_halos(): return [lax.ppermute(edges[0], 'sec', sib_pairs)]  2.33 us
  transfers between devices with their start and end apart: 17, of which 5 were waited for; matrix products, arithmetic and copies ran while one was open for 4% of the time, Pallas kernels for 3%

profile of v1, /device:TPU:0, one launch (start us, length us, event | category | flops | bytes accessed | tf_op | source)
XLA Modules:
  0.0 72.4 jit_solution(15895521625600252755)
XLA Ops:
  0.7 1.9 %shard_map.139 = (f32[12,4,8,128]{3,2,1,0:T(8,128)}, f32[12,4,8,128]{3,2,1,0:T(8,128)}) custom-call(f32[4,64,128]{2,1,0:T(8,128)} %bitcast.9, f32[4,64,128]{2,1,0:T(8,128)} %bitcast.10, f32[64,128]{1,0:T(8,128)} %bitcast.13, f32[64,128]{1,0:T(8,128)} %bitcast.14, f32[64,128]{1,0:T(8,128)} %bitcast.15, f32[64,128]{1,0:T(8,128)} %bitcast.16), custom_call_target="tpu_custom_call" | custom-call | flops 100000 | bytes 1000000 | tf_op jit(solution)/shard_map/pallas_call | solution.py:415
  3.1 1.3 %collective-permute-done.17.got = f32[12,4,8,128]{3,2,1,0:T(8,128)S(1)} collective-permute-done((f32[12,4,8,128]{3,2,1,0:T(8,128)}, f32[12,4,8,128]{3,2,1,0:T(8,128)S(1)}, u32[]{:S(2)}, u32[]{:S(2)}) %collective-permute-start.17) | collective-permute-done | bytes 196640 | tf_op jit(solution)/shard_map/ppermute | solution.py:399
  5.1 1.8 %shard_map.140 = (f32[12,4,8,256]{3,2,1,0:T(8,128)S(1)}, f32[6,4,8,256]{3,2,1,0:T(8,128)}) custom-call(f32[12,4,8,128]{3,2,1,0:T(8,128)} %get-tuple-element.77.keep, f32[12,4,8,128]{3,2,1,0:T(8,128)} %copy-done.1), custom_call_target="tpu_custom_call" | custom-call | flops 100000 | bytes 1000000 | tf_op jit(solution)/shard_map/pallas_call | solution.py:427
  6.8 2.8 %collective-permute-start.18 = (f32[6,4,8,256]{3,2,1,0:T(8,128)}, f32[6,4,8,256]{3,2,1,0:T(8,128)S(1)}, u32[]{:S(2)}, u32[]{:S(2)}) collective-permute-start(f32[6,4,8,256]{3,2,1,0:T(8,128)} %get-tuple-element.80), channel_id=1, source_target_pairs={{0,2},{2,0},{1,3},{3,1},{4,6},{6,4},{5,7},{7,5},{8,10},{10,8},{9,1... | collective-permute-start | bytes 589832 | tf_op jit(solution)/shard_map/ppermute | solution.py:406
  10.4 3.0 %collective-permute-start.19 = (f32[12,4,8,256]{3,2,1,0:T(8,128)S(1)}, f32[12,4,8,256]{3,2,1,0:T(8,128)S(1)}, u32[]{:S(2)}, u32[]{:S(2)}) collective-permute-start(f32[12,4,8,256]{3,2,1,0:T(8,128)S(1)} %get-tuple-element.79.refs_3_.refs_9_), channel_id=1, source_target_pairs={{0,1},{1,0},{2,3},{3,2},{4,5},{5,4},{6,7},{7,6},{8,9},{9,8},{10,11... | collective-permute-start | bytes 1179656 | tf_op jit(solution)/shard_map/ppermute | solution.py:399
  13.3 1.8 %collective-permute-done.18.refs_4_.refs_10_ = f32[6,4,8,256]{3,2,1,0:T(8,128)S(1)} collective-permute-done((f32[6,4,8,256]{3,2,1,0:T(8,128)}, f32[6,4,8,256]{3,2,1,0:T(8,128)S(1)}, u32[]{:S(2)}, u32[]{:S(2)}) %collective-permute-start.18) | collective-permute-done | bytes 196640 | tf_op jit(solution)/shard_map/ppermute | solution.py:406
  15.8 3.2 %collective-permute-start.20 = (f32[6,4,8,256]{3,2,1,0:T(8,128)S(1)}, f32[6,4,8,256]{3,2,1,0:T(8,128)S(1)}, u32[]{:S(2)}, u32[]{:S(2)}) collective-permute-start(f32[6,4,8,256]{3,2,1,0:T(8,128)S(1)} %collective-permute-done.18.refs_4_.refs_10_), channel_id=1, source_target_pairs={{0,1},{1,0},{2,3},{3,2},{4,5},{5,4},{6,7},{7,6},{8,9},{9,8},{10,11... | collective-permute-start | bytes 589832 | tf_op jit(solution)/shard_map/ppermute | solution.py:399
  19.0 1.5 %copy.15.pos = s32[256,3]{1,0:T(8,128)} copy(s32[256,3]{0,1:T(4,128)} %param.22) | data formatting | bytes 6144 | tf_op args[8]
  20.5 1.9 %shard_map.141.refs_15_ = f32[9,12,16,256]{3,2,1,0:T(8,128)S(1)} custom-call(s32[256,3]{1,0:T(8,128)} %copy.15.pos, s32[3,256]{1,0:T(4,128)} %bitcast.17, f32[9,256]{1,0:T(8,128)} %data.1), custom_call_target="tpu_custom_call" | custom-call | flops 100000 | bytes 1000000 | tf_op jit(solution)/shard_map/pallas_call | solution.py:436
  22.4 6.8 %shard_map.142 = (f32[8,4,8,256]{3,2,1,0:T(8,128)}, bf16[3,4,16,256]{3,2,1,0:T(8,128)(2,1)}, f32[4,4,8,256]{3,2,1,0:T(8,128)}) custom-call(s32[3]{0:T(128)S(1)} %copy-done.19, f32[9]{0:T(128)S(1)} %copy-done.20, s32[3]{0:T(128)S(1)} %copy-done.21, f32[12,4,8,256]{3,2,1,0:T(8,128)S(1)} %get-tuple-element.79.refs_3_.refs_9_, ...), custom_call_target="tpu_custom_call" | custom-call | flops 10000000 | bytes 3000000 | tf_op jit(solution)/shard_map/pallas_call | solution.py:479
  29.2 1.5 %collective-permute-start.23 = (f32[4,4,8,256]{3,2,1,0:T(8,128)}, f32[4,4,8,256]{3,2,1,0:T(8,128)}, u32[]{:S(2)}, u32[]{:S(2)}) collective-permute-start(f32[4,4,8,256]{3,2,1,0:T(8,128)} %get-tuple-element.82), channel_id=1, source_target_pairs={{0,2},{2,0},{1,3},{3,1},{4,6},{6,4},{5,7},{7,5},{8,10},{10,8},{9,1... | collective-permute-start | bytes 393224 | tf_op jit(solution)/shard_map/ppermute | solution.py:406
  30.7 1.4 %collective-permute-start.26 = (f32[8,4,8,256]{3,2,1,0:T(8,128)}, f32[8,4,8,256]{3,2,1,0:T(8,128)}, u32[]{:S(2)}, u32[]{:S(2)}) collective-permute-start(f32[8,4,8,256]{3,2,1,0:T(8,128)} %get-tuple-element.81.refs_3_), channel_id=1, source_target_pairs={{1,4},{4,1},{5,8},{8,5},{9,12},{12,9},{3,6},{6,3},{7,10},{10,7},{1... | collective-permute-start | bytes 786440 | tf_op jit(solution)/shard_map/ppermute | solution.py:402
  32.0 2.3 %collective-permute-start.24 = (f32[8,4,8,256]{3,2,1,0:T(8,128)}, f32[8,4,8,256]{3,2,1,0:T(8,128)}, u32[]{:S(2)}, u32[]{:S(2)}) collective-permute-start(f32[8,4,8,256]{3,2,1,0:T(8,128)} %get-tuple-element.81.refs_3_), channel_id=1, source_target_pairs={{0,1},{1,0},{2,3},{3,2},{4,5},{5,4},{6,7},{7,6},{8,9},{9,8},{10,11... | collective-permute-start | bytes 786440 | tf_op jit(solution)/shard_map/ppermute | solution.py:399
  34.9 1.3 %collective-permute-start.27 = (f32[4,4,8,256]{3,2,1,0:T(8,128)}, f32[4,4,8,256]{3,2,1,0:T(8,128)}, u32[]{:S(2)}, u32[]{:S(2)}) collective-permute-start(f32[4,4,8,256]{3,2,1,0:T(8,128)} %collective-permute-done.23.refs_4_), channel_id=1, source_target_pairs={{1,4},{4,1},{5,8},{8,5},{9,12},{12,9},{3,6},{6,3},{7,10},{10,7},{1... | collective-permute-start | bytes 393224 | tf_op jit(solution)/shard_map/ppermute | solution.py:402
  36.2 2.4 %collective-permute-start.25 = (f32[4,4,8,256]{3,2,1,0:T(8,128)}, f32[4,4,8,256]{3,2,1,0:T(8,128)}, u32[]{:S(2)}, u32[]{:S(2)}) collective-permute-start(f32[4,4,8,256]{3,2,1,0:T(8,128)} %collective-permute-done.23.refs_4_), channel_id=1, source_target_pairs={{0,1},{1,0},{2,3},{3,2},{4,5},{5,4},{6,7},{7,6},{8,9},{9,8},{10,11... | collective-permute-start | bytes 393224 | tf_op jit(solution)/shard_map/ppermute | solution.py:399
  40.0 4.5 %shard_map.143 = (f32[8,4,8,256]{3,2,1,0:T(8,128)}, bf16[3,4,16,256]{3,2,1,0:T(8,128)(2,1)}, f32[4,4,8,256]{3,2,1,0:T(8,128)}, f32[8,4,8,128]{3,2,1,0:T(8,128)}) custom-call(s32[3]{0:T(128)S(1)} %copy-done.19, f32[9]{0:T(128)S(1)} %copy-done.20, s32[3]{0:T(128)S(1)} %copy-done.21, f32[8,4,8,256]{3,2,1,0:T(8,128)} %get-tuple-element.81.refs_3_, ...), custom_call_target="tpu_custom_call" | custom-call | flops 10000000 | bytes 3000000 | tf_op jit(solution)/shard_map/pallas_call | solution.py:479
  44.5 27.0 %conditional.1 = ((bf16[48,8,8,128]{3,2,1,0:T(8,128)(2,1)}, f32[256,128]{1,0:T(8,128)}, f32[256,128]{1,0:T(8,128)}), (bf16[48,8,8,128]{3,2,1,0:T(8,128)(2,1)S(1)}, f32[256,128]{1,0:T(8,128)S(1)}, f32[256,128]{1,0:T(8,128)S(1)})) conditional(s32[]{:T(128)} %convert_element_type.3, (f32[8,4,8,128]{3,2,1,0:T(8,128)}, bf16[3,4,16,256]{3,2,1,0:T(8,128)(2,1)}, ...), branch_computations={%region_1.0_spmd, %region_2.0_spmd} | conditional | flops 10100000 | bytes 16322268 | solution.py:527
  44.5 1.6 %collective-permute-start.1 = (bf16[3,4,16,256]{3,2,1,0:T(8,128)(2,1)}, bf16[3,4,16,256]{3,2,1,0:T(8,128)(2,1)S(1)}, u32[]{:S(2)}, u32[]{:S(2)}) collective-permute-start(bf16[3,4,16,256]{3,2,1,0:T(8,128)(2,1)} %get-tuple-element.39.snaps), channel_id=1, source_target_pairs={{0,1},{1,0},{2,3},{3,2},{4,5},{5,4},{6,7},{7,6},{8,9},{9,8},{10,11... | collective-permute-start | bytes 294920 | tf_op jit(solution)/shard_map/cond/branch_0_fun/ppermute | solution.py:399
  47.9 4.0 %collective-permute-start = (f32[8,4,8,128]{3,2,1,0:T(8,128)}, f32[8,4,8,128]{3,2,1,0:T(8,128)S(1)}, u32[]{:S(2)}, u32[]{:S(2)}) collective-permute-start(f32[8,4,8,128]{3,2,1,0:T(8,128)} %get-tuple-element.38), channel_id=1, source_target_pairs={{0,1},{1,0},{2,3},{3,2},{4,5},{5,4},{6,7},{7,6},{8,9},{9,8},{10,11... | collective-permute-start | bytes 393224 | tf_op jit(solution)/shard_map/cond/branch_0_fun/ppermute | solution.py:399
  52.4 3.5 %collective-permute-start.5 = (bf16[3,4,16,256]{3,2,1,0:T(8,128)(2,1)S(1)}, bf16[3,4,16,256]{3,2,1,0:T(8,128)(2,1)S(1)}, u32[]{:S(2)}, u32[]{:S(2)}) collective-permute-start(bf16[3,4,16,256]{3,2,1,0:T(8,128)(2,1)S(1)} %collective-permute-done.3.far), channel_id=1, source_target_pairs={{0,1},{1,0},{2,3},{3,2},{4,5},{5,4},{6,7},{7,6},{8,9},{9,8},{10,11... | collective-permute-start | bytes 294920 | tf_op jit(solution)/shard_map/cond/branch_0_fun/ppermute | solution.py:399
  57.4 11.1 %branch_0_fun.1 = (bf16[48,8,8,128]{3,2,1,0:T(8,128)(2,1)}, f32[256,128]{1,0:T(8,128)}, f32[256,128]{1,0:T(8,128)}) custom-call(s32[48,2]{1,0:T(8,128)} %copy.16.lags, f32[8,4,8,256]{3,2,1,0:T(8,128)} %get-tuple-element.37.own, f32[8,4,8,128]{3,2,1,0:T(8,128)} %copy-done.4, bf16[3,4,16,256]{3,2,1,0:T(8,128)(2,1)} %get-tuple-element.39.snaps, ...), custom_call_target="tpu_custom_call" | custom-call | flops 100000 | bytes 1000000 | tf_op jit(solution)/shard_map/cond/branch_0_fun/pallas_call | solution.py:506
  68.5 1.1 %copy.36 = bf16[48,8,8,128]{3,2,1,0:T(8,128)(2,1)S(1)} copy(bf16[48,8,8,128]{3,2,1,0:T(8,128)(2,1)} %get-tuple-element.148) | data formatting | bytes 1572864 | tf_op jit(solution)/shard_map/cond
  69.6 0.9 %copy.37 = f32[256,128]{1,0:T(8,128)S(1)} copy(f32[256,128]{1,0:T(8,128)} %get-tuple-element.149) | data formatting | bytes 262144 | tf_op jit(solution)/shard_map/cond
  70.5 0.9 %copy.38 = f32[256,128]{1,0:T(8,128)S(1)} copy(f32[256,128]{1,0:T(8,128)} %get-tuple-element.150) | data formatting | bytes 262144 | tf_op jit(solution)/shard_map/cond
  (51 shorter events, 8.6 us)
Async XLA Ops:
  0.6 21.8 %copy-start.19 = (s32[3]{0:T(128)S(1)}, s32[3]{0:T(128)}, u32[]{:S(2)}) copy-start(s32[3]{0:T(128)} %refs_0_.3) | copy-start | bytes 40
  0.6 21.8 %copy-start.20 = (f32[9]{0:T(128)S(1)}, f32[9]{0:T(128)}, u32[]{:S(2)}) copy-start(f32[9]{0:T(128)} %refs_1_.3) | copy-start | bytes 112
  0.7 21.8 %copy-start.21 = (s32[3]{0:T(128)S(1)}, s32[3]{0:T(128)}, u32[]{:S(2)}) copy-start(s32[3]{0:T(128)} %refs_2_.3) | copy-start | bytes 40
  2.6 1.8 %collective-permute-start.17 = (f32[12,4,8,128]{3,2,1,0:T(8,128)}, f32[12,4,8,128]{3,2,1,0:T(8,128)S(1)}, u32[]{:S(2)}, u32[]{:S(2)}) collective-permute-start(f32[12,4,8,128]{3,2,1,0:T(8,128)} %get-tuple-element.78), channel_id=1, source_target_pairs={{0,1},{1,0},{2,3},{3,2},{4,5},{5,4},{6,7},{7,6},{8,9},{9,8},{10,11... | collective-permute-start | bytes 589832 | tf_op jit(solution)/shard_map/ppermute | solution.py:399
  6.8 8.3 %collective-permute-start.18 = (f32[6,4,8,256]{3,2,1,0:T(8,128)}, f32[6,4,8,256]{3,2,1,0:T(8,128)S(1)}, u32[]{:S(2)}, u32[]{:S(2)}) collective-permute-start(f32[6,4,8,256]{3,2,1,0:T(8,128)} %get-tuple-element.80), channel_id=1, source_target_pairs={{0,2},{2,0},{1,3},{3,1},{4,6},{6,4},{5,7},{7,5},{8,10},{10,8},{9,1... | collective-permute-start | bytes 589832 | tf_op jit(solution)/shard_map/ppermute | solution.py:406
  9.7 12.7 %collective-permute-start.21 = (f32[12,4,8,256]{3,2,1,0:T(8,128)S(1)}, f32[12,4,8,256]{3,2,1,0:T(8,128)S(1)}, u32[]{:S(2)}, u32[]{:S(2)}) collective-permute-start(f32[12,4,8,256]{3,2,1,0:T(8,128)S(1)} %get-tuple-element.79.refs_3_.refs_9_), channel_id=1, source_target_pairs={{1,4},{4,1},{5,8},{8,5},{9,12},{12,9},{3,6},{6,3},{7,10},{10,7},{1... | collective-permute-start | bytes 1179656 | tf_op jit(solution)/shard_map/ppermute | solution.py:402
  10.4 12.0 %collective-permute-start.19 = (f32[12,4,8,256]{3,2,1,0:T(8,128)S(1)}, f32[12,4,8,256]{3,2,1,0:T(8,128)S(1)}, u32[]{:S(2)}, u32[]{:S(2)}) collective-permute-start(f32[12,4,8,256]{3,2,1,0:T(8,128)S(1)} %get-tuple-element.79.refs_3_.refs_9_), channel_id=1, source_target_pairs={{0,1},{1,0},{2,3},{3,2},{4,5},{5,4},{6,7},{7,6},{8,9},{9,8},{10,11... | collective-permute-start | bytes 1179656 | tf_op jit(solution)/shard_map/ppermute | solution.py:399
  15.1 7.3 %collective-permute-start.22 = (f32[6,4,8,256]{3,2,1,0:T(8,128)S(1)}, f32[6,4,8,256]{3,2,1,0:T(8,128)S(1)}, u32[]{:S(2)}, u32[]{:S(2)}) collective-permute-start(f32[6,4,8,256]{3,2,1,0:T(8,128)S(1)} %collective-permute-done.18.refs_4_.refs_10_), channel_id=1, source_target_pairs={{1,4},{4,1},{5,8},{8,5},{9,12},{12,9},{3,6},{6,3},{7,10},{10,7},{1... | collective-permute-start | bytes 589832 | tf_op jit(solution)/shard_map/ppermute | solution.py:402
  15.8 6.6 %collective-permute-start.20 = (f32[6,4,8,256]{3,2,1,0:T(8,128)S(1)}, f32[6,4,8,256]{3,2,1,0:T(8,128)S(1)}, u32[]{:S(2)}, u32[]{:S(2)}) collective-permute-start(f32[6,4,8,256]{3,2,1,0:T(8,128)S(1)} %collective-permute-done.18.refs_4_.refs_10_), channel_id=1, source_target_pairs={{0,1},{1,0},{2,3},{3,2},{4,5},{5,4},{6,7},{7,6},{8,9},{9,8},{10,11... | collective-permute-start | bytes 589832 | tf_op jit(solution)/shard_map/ppermute | solution.py:399
  29.2 5.7 %collective-permute-start.23 = (f32[4,4,8,256]{3,2,1,0:T(8,128)}, f32[4,4,8,256]{3,2,1,0:T(8,128)}, u32[]{:S(2)}, u32[]{:S(2)}) collective-permute-start(f32[4,4,8,256]{3,2,1,0:T(8,128)} %get-tuple-element.82), channel_id=1, source_target_pairs={{0,2},{2,0},{1,3},{3,1},{4,6},{6,4},{5,7},{7,5},{8,10},{10,8},{9,1... | collective-permute-start | bytes 393224 | tf_op jit(solution)/shard_map/ppermute | solution.py:406
  30.7 9.3 %collective-permute-start.26 = (f32[8,4,8,256]{3,2,1,0:T(8,128)}, f32[8,4,8,256]{3,2,1,0:T(8,128)}, u32[]{:S(2)}, u32[]{:S(2)}) collective-permute-start(f32[8,4,8,256]{3,2,1,0:T(8,128)} %get-tuple-element.81.refs_3_), channel_id=1, source_target_pairs={{1,4},{4,1},{5,8},{8,5},{9,12},{12,9},{3,6},{6,3},{7,10},{10,7},{1... | collective-permute-start | bytes 786440 | tf_op jit(solution)/shard_map/ppermute | solution.py:402
  32.0 7.9 %collective-permute-start.24 = (f32[8,4,8,256]{3,2,1,0:T(8,128)}, f32[8,4,8,256]{3,2,1,0:T(8,128)}, u32[]{:S(2)}, u32[]{:S(2)}) collective-permute-start(f32[8,4,8,256]{3,2,1,0:T(8,128)} %get-tuple-element.81.refs_3_), channel_id=1, source_target_pairs={{0,1},{1,0},{2,3},{3,2},{4,5},{5,4},{6,7},{7,6},{8,9},{9,8},{10,11... | collective-permute-start | bytes 786440 | tf_op jit(solution)/shard_map/ppermute | solution.py:399
  34.9 5.0 %collective-permute-start.27 = (f32[4,4,8,256]{3,2,1,0:T(8,128)}, f32[4,4,8,256]{3,2,1,0:T(8,128)}, u32[]{:S(2)}, u32[]{:S(2)}) collective-permute-start(f32[4,4,8,256]{3,2,1,0:T(8,128)} %collective-permute-done.23.refs_4_), channel_id=1, source_target_pairs={{1,4},{4,1},{5,8},{8,5},{9,12},{12,9},{3,6},{6,3},{7,10},{10,7},{1... | collective-permute-start | bytes 393224 | tf_op jit(solution)/shard_map/ppermute | solution.py:402
  36.2 3.7 %collective-permute-start.25 = (f32[4,4,8,256]{3,2,1,0:T(8,128)}, f32[4,4,8,256]{3,2,1,0:T(8,128)}, u32[]{:S(2)}, u32[]{:S(2)}) collective-permute-start(f32[4,4,8,256]{3,2,1,0:T(8,128)} %collective-permute-done.23.refs_4_), channel_id=1, source_target_pairs={{0,1},{1,0},{2,3},{3,2},{4,5},{5,4},{6,7},{7,6},{8,9},{9,8},{10,11... | collective-permute-start | bytes 393224 | tf_op jit(solution)/shard_map/ppermute | solution.py:399
  40.0 4.5 %copy-start.22 = (s32[48,2]{0,1:T(2,128)S(1)}, s32[48,2]{0,1:T(2,128)}, u32[]{:S(2)}) copy-start(s32[48,2]{0,1:T(2,128)} %param.25) | copy-start | bytes 1156
  44.5 2.8 %collective-permute-start.1 = (bf16[3,4,16,256]{3,2,1,0:T(8,128)(2,1)}, bf16[3,4,16,256]{3,2,1,0:T(8,128)(2,1)S(1)}, u32[]{:S(2)}, u32[]{:S(2)}) collective-permute-start(bf16[3,4,16,256]{3,2,1,0:T(8,128)(2,1)} %get-tuple-element.39.snaps), channel_id=1, source_target_pairs={{0,1},{1,0},{2,3},{3,2},{4,5},{5,4},{6,7},{7,6},{8,9},{9,8},{10,11... | collective-permute-start | bytes 294920 | tf_op jit(solution)/shard_map/cond/branch_0_fun/ppermute | solution.py:399
  46.1 5.8 %collective-permute-start.2 = (bf16[3,4,16,256]{3,2,1,0:T(8,128)(2,1)}, bf16[3,4,16,256]{3,2,1,0:T(8,128)(2,1)S(1)}, u32[]{:S(2)}, u32[]{:S(2)}) collective-permute-start(bf16[3,4,16,256]{3,2,1,0:T(8,128)(2,1)} %get-tuple-element.39.snaps), channel_id=1, source_target_pairs={{1,4},{4,1},{5,8},{8,5},{9,12},{12,9},{3,6},{6,3},{7,10},{10,7},{1... | collective-permute-start | bytes 294920 | tf_op jit(solution)/shard_map/cond/branch_0_fun/ppermute | solution.py:402
  47.3 9.5 %copy-start.11 = (bf16[3,4,16,256]{3,2,1,0:T(8,128)(2,1)}, bf16[3,4,16,256]{3,2,1,0:T(8,128)(2,1)S(1)}, u32[]{:S(2)}) copy-start(bf16[3,4,16,256]{3,2,1,0:T(8,128)(2,1)S(1)} %collective-permute-done.1.sib) | copy-start | bytes 294916 | tf_op jit(solution)/shard_map/cond
  47.3 5.1 %collective-permute-start.3 = (bf16[3,4,16,256]{3,2,1,0:T(8,128)(2,1)S(1)}, bf16[3,4,16,256]{3,2,1,0:T(8,128)(2,1)S(1)}, u32[]{:S(2)}, u32[]{:S(2)}) collective-permute-start(bf16[3,4,16,256]{3,2,1,0:T(8,128)(2,1)S(1)} %collective-permute-done.1.sib), channel_id=1, source_target_pairs={{1,4},{4,1},{5,8},{8,5},{9,12},{12,9},{3,6},{6,3},{7,10},{10,7},{1... | collective-permute-start | bytes 294920 | tf_op jit(solution)/shard_map/cond/branch_0_fun/ppermute | solution.py:402
  47.9 8.6 %collective-permute-start = (f32[8,4,8,128]{3,2,1,0:T(8,128)}, f32[8,4,8,128]{3,2,1,0:T(8,128)S(1)}, u32[]{:S(2)}, u32[]{:S(2)}) collective-permute-start(f32[8,4,8,128]{3,2,1,0:T(8,128)} %get-tuple-element.38), channel_id=1, source_target_pairs={{0,1},{1,0},{2,3},{3,2},{4,5},{5,4},{6,7},{7,6},{8,9},{9,8},{10,11... | collective-permute-start | bytes 393224 | tf_op jit(solution)/shard_map/cond/branch_0_fun/ppermute | solution.py:399
  51.9 4.9 %copy-start.12 = (bf16[3,4,16,256]{3,2,1,0:T(8,128)(2,1)}, bf16[3,4,16,256]{3,2,1,0:T(8,128)(2,1)S(1)}, u32[]{:S(2)}) copy-start(bf16[3,4,16,256]{3,2,1,0:T(8,128)(2,1)S(1)} %collective-permute-done.2.near) | copy-start | bytes 294916 | tf_op jit(solution)/shard_map/cond
  51.9 4.6 %collective-permute-start.4 = (bf16[3,4,16,256]{3,2,1,0:T(8,128)(2,1)S(1)}, bf16[3,4,16,256]{3,2,1,0:T(8,128)(2,1)S(1)}, u32[]{:S(2)}, u32[]{:S(2)}) collective-permute-start(bf16[3,4,16,256]{3,2,1,0:T(8,128)(2,1)S(1)} %collective-permute-done.2.near), channel_id=1, source_target_pairs={{0,1},{1,0},{2,3},{3,2},{4,5},{5,4},{6,7},{7,6},{8,9},{9,8},{10,11... | collective-permute-start | bytes 294920 | tf_op jit(solution)/shard_map/cond/branch_0_fun/ppermute | solution.py:399
  52.4 4.4 %copy-start.14 = (bf16[3,4,16,256]{3,2,1,0:T(8,128)(2,1)}, bf16[3,4,16,256]{3,2,1,0:T(8,128)(2,1)S(1)}, u32[]{:S(2)}) copy-start(bf16[3,4,16,256]{3,2,1,0:T(8,128)(2,1)S(1)} %collective-permute-done.3.far) | copy-start | bytes 294916 | tf_op jit(solution)/shard_map/cond
  52.4 4.4 %collective-permute-start.5 = (bf16[3,4,16,256]{3,2,1,0:T(8,128)(2,1)S(1)}, bf16[3,4,16,256]{3,2,1,0:T(8,128)(2,1)S(1)}, u32[]{:S(2)}, u32[]{:S(2)}) collective-permute-start(bf16[3,4,16,256]{3,2,1,0:T(8,128)(2,1)S(1)} %collective-permute-done.3.far), channel_id=1, source_target_pairs={{0,1},{1,0},{2,3},{3,2},{4,5},{5,4},{6,7},{7,6},{8,9},{9,8},{10,11... | collective-permute-start | bytes 294920 | tf_op jit(solution)/shard_map/cond/branch_0_fun/ppermute | solution.py:399
  (7 other events, 5.4 us)
